TPU v7x, 256 devices: a whole 4x4x8 slice. The times are simulated.
256 devices in a mesh: mode: 16 (over z, core), cols: 16 (over x, y).
Axes of the slice: x: 4, y: 4, z: 8, core: 2. Of those that a mesh axis runs over, the one named last changes fastest.
Arguments:
- snapshots: float32 [512, 262144], P('mode', 'cols'), may hold values from -54 to 54, as said below
- start_basis: float32 [512, 128], replicated, may hold values from -6 to 6
Outputs:
- subspace_basis: float32 [512, 128], replicated
- core_tensor: float32 [128, 262144], P('mode', 'cols')
Inputs may be any that keep to these rules, and one draw needn't show every extreme that they name: `snapshots`: entries are finite real values.
All inputs are finite; a program needn't handle non-finite values.
Results may differ from a plain program's by a relative error of at most 0.00017.
Values sent between devices are 32-bit elements; how exact they have to be, the bound alone decides.
No kernel may reach another device: no remote copies, remote signals or barrier semaphores. Data moves between devices by JAX's collectives and lax.ppermute only.
A program may use at most 64 MiB of HBM per device.

v0:
```python
import jax
import jax.numpy as jnp
from jax import lax
from jax.sharding import Mesh
from jax.sharding import PartitionSpec as P

MODE = ("mode_0", "mode_1")
COLS = ("cols_0", "cols_1")


def cut_along(value, dim, size):
    shape = value.shape
    parts = value.reshape(*shape[:dim], size, shape[dim] // size, *shape[dim + 1 :])
    return jnp.moveaxis(parts, dim, 0)


def sent_and_summed(value, axis, dim):
    size = lax.axis_size(axis)
    parts = lax.all_to_all(cut_along(value, dim, size), axis, 0, 0, tiled=True)
    return jnp.sum(parts, axis=0)


def sum_by_axis(value, axes, dim):
    far, near = axes
    parts = cut_along(value, dim, lax.axis_size(far))
    nearer = sent_and_summed(parts, near, dim + 1)
    arrived = lax.all_to_all(nearer, far, split_axis=0, concat_axis=0, tiled=True)
    return arrived.sum(axis=0)


def padded_to(lines, size):
    spare = -lines.shape[0] % size
    if not spare:
        return lines
    return jnp.concatenate([lines, jnp.zeros((spare, *lines.shape[1:]), lines.dtype)])


def from_everyone(value, axis):
    copies = jnp.broadcast_to(value, (lax.axis_size(axis), *value.shape))
    return lax.all_to_all(copies, axis, split_axis=0, concat_axis=0, tiled=True)


def joined_along(parts, dim):
    parts = jnp.moveaxis(parts, 0, dim)
    shape = parts.shape
    return parts.reshape(*shape[:dim], shape[dim] * shape[dim + 1], *shape[dim + 2 :])


def whole_of(value, axes, dim):
    far, near = axes
    leading = from_everyone(value, far)
    parts = jnp.swapaxes(from_everyone(leading, near), 0, 1)
    return joined_along(parts.reshape(-1, *value.shape), dim)


def nested_sum(value, axes):
    lines = value.reshape(-1, value.shape[-1])
    own = sum_by_axis(padded_to(lines, lax.axis_size(axes[0]) * lax.axis_size(axes[1])), axes, 0)
    whole = whole_of(own, axes, 0)
    return whole[: len(lines)].reshape(value.shape)


def orthonormal(projected):
    current = projected
    for sweep in range(2):
        inner = jnp.dot(
            current.T, current, precision=lax.Precision.HIGHEST, preferred_element_type=jnp.float32
        )
        lower_part = jnp.linalg.cholesky(inner)
        current = jax.scipy.linalg.solve_triangular(lower_part, current.T, lower=True).T
    return current


def shards(snapshots, start_basis):
    fibres = lax.all_to_all(snapshots, MODE, split_axis=1, concat_axis=0, tiled=True)
    along_cols = jnp.dot(
        fibres.T, start_basis, precision=lax.Precision.HIGHEST, preferred_element_type=jnp.float32
    )
    partial_term = jnp.dot(
        fibres, along_cols, precision=lax.Precision.HIGHEST, preferred_element_type=jnp.float32
    )
    projected = nested_sum(partial_term, (("mode_0", "mode_1", "cols_0"), "cols_1"))
    subspace_basis = orthonormal(projected)
    core_local = jnp.dot(
        subspace_basis.T,
        fibres,
        precision=lax.Precision.HIGHEST,
        preferred_element_type=jnp.float32,
    )
    core_tensor = lax.all_to_all(core_local, MODE, split_axis=0, concat_axis=1, tiled=True)
    return (subspace_basis, core_tensor)


def solution(mesh):
    finer = Mesh(mesh.devices.reshape(8, 2, 4, 4), ("mode_0", "mode_1", "cols_0", "cols_1"))
    return jax.shard_map(
        shards,
        mesh=finer,
        in_specs=(P(MODE, COLS), P()),
        out_specs=(P(), P(MODE, COLS)),
        check_vma=False,
    )
```

profile of v0, /device:TPU:1, one launch (start us, length us, event | category | flops | bytes accessed | tf_op | source)
XLA Modules:
  0.0 191.6 jit_solution(16109052127622031826)
XLA Ops:
  0.6 0.0 copy-start
  0.6 1.8 copy.43
  2.4 60.7 %all_to_all.55 = f32[32,16,1024]{2,0,1:T(8,128)S(1)} all-to-all(f32[32,16,1024]{2,0,1:T(8,128)S(1)} %bitcast.61), channel_id=1, replica_groups=mesh['mode_0'=8,'mode_1'=2,'cols_0'=4,'cols_1'=4] {'mode_0','mode_1'}, dimensions={1} | all-to-all | bytes 4194304 | tf_op jit(solution)/shard_map/all_to_all | solution.py:75
  63.1 0.0 copy-done
  63.1 3.4 %fusion.13 = f32[1024,128]{1,0:T(8,128)S(1)} fusion(f32[512,1024]{1,0:T(8,128)S(1)} %bitcast.58, f32[512,128]{1,0:T(8,128)S(1)} %copy-done), kind=kOutput, calls=%fused_computation.25 | convolution fusion | flops 805306368 | bytes 2883584 | tf_op jit(solution)/shard_map/dot_general | solution.py:76
  66.5 2.3 %convolution_bitcast_fusion = f32[512,128]{0,1:T(8,128)S(1)} fusion(f32[1024,128]{1,0:T(8,128)S(1)} %fusion.13, f32[512,1024]{1,0:T(8,128)S(1)} %bitcast.59), kind=kOutput, calls=%fused_computation.1 | convolution fusion | flops 805306368 | bytes 2883584 | tf_op jit(solution)/shard_map/dot_general | solution.py:79
  68.9 0.1 copy.31
  69.0 0.1 copy.32
  69.1 10.5 %all_to_all.56 = f32[4,64,2,128]{3,2,1,0:T(2,128)S(1)} all-to-all(f32[4,64,2,128]{3,2,1,0:T(2,128)S(1)} %copy.32), channel_id=1, replica_groups=mesh['mode_0'=8,'mode_1'=2,'cols_0'=4,'cols_1'=4] {'cols_1'}, dimensions={0} | all-to-all | bytes 524288 | tf_op jit(solution)/shard_map/all_to_all | solution.py:19
  79.6 0.1 reduce_sum.18
  79.7 15.8 %all_to_all.57 = f32[64,2,128]{2,1,0:T(2,128)S(1)} all-to-all(f32[64,2,128]{2,1,0:T(2,128)S(1)} %reduce_sum.18), channel_id=1, replica_groups=mesh['mode_0'=8,'mode_1'=2,'cols_0'=4,'cols_1'=4] {'mode_0','mode_1','co..., dimensions={0} | all-to-all | bytes 131072 | tf_op jit(solution)/shard_map/all_to_all | solution.py:27
  95.5 0.1 reduce_sum.19
  95.6 13.9 %all_to_all.58 = f32[64,2,128]{2,1,0:T(2,128)S(1)} all-to-all(f32[64,2,128]{2,1,0:T(2,128)S(1)} %broadcast_in_dim.7), channel_id=1, replica_groups=mesh['mode_0'=8,'mode_1'=2,'cols_0'=4,'cols_1'=4] {'mode_0','mode_1','co..., dimensions={0} | all-to-all | bytes 131072 | tf_op jit(solution)/shard_map/all_to_all | solution.py:40
  109.5 7.9 %all_to_all.59 = f32[4,64,2,128]{3,1,2,0:T(8,128)S(1)} all-to-all(f32[4,64,2,128]{3,1,2,0:T(8,128)S(1)} %broadcast_in_dim.8), channel_id=1, replica_groups=mesh['mode_0'=8,'mode_1'=2,'cols_0'=4,'cols_1'=4] {'cols_1'}, dimensions={0} | all-to-all | bytes 524288 | tf_op jit(solution)/shard_map/all_to_all | solution.py:40
  117.4 0.6 convolution_bitcast_fusion.1
  118.0 0.1 copy.35
  118.1 11.7 %cholesky.44 = f32[128,128]{1,0:T(8,128)S(1)} custom-call(f32[128,128]{1,0:T(8,128)S(1)} %fusion.9), custom_call_target="Cholesky" | custom-call | tf_op jit(solution)/shard_map/jit(cholesky)/cholesky | solution.py:69
  129.9 0.6 compare_reduce_fusion.1
  130.5 0.7 fusion.2
  131.2 9.8 %custom-call.6 = f32[1,128,128]{1,2,0:T(8,128)S(1)} custom-call(f32[1,128,128]{2,1,0:T(8,128)S(1)} %fusion.2), custom_call_target="InvertDiagBlocksLowerTriangular" | custom-call | tf_op jit(solution)/shard_map/jit(_solve_triangular)/triangular_solve | solution.py:70
  141.0 0.2 copy.36
  141.2 0.4 fusion.7
  141.6 0.4 fusion.14
  142.0 0.1 copy.37
  142.1 11.7 %cholesky.55 = f32[128,128]{1,0:T(8,128)S(1)} custom-call(f32[128,128]{1,0:T(8,128)S(1)} %fusion.6), custom_call_target="Cholesky" | custom-call | tf_op jit(solution)/shard_map/jit(cholesky)/cholesky | solution.py:69
  153.9 0.6 compare_reduce_fusion
  154.5 0.7 fusion.3
  155.2 10.0 %custom-call.7 = f32[1,128,128]{1,2,0:T(8,128)S(1)} custom-call(f32[1,128,128]{2,1,0:T(8,128)S(1)} %fusion.3), custom_call_target="InvertDiagBlocksLowerTriangular" | custom-call | tf_op jit(solution)/shard_map/jit(_solve_triangular)/triangular_solve | solution.py:70
  165.2 0.4 fusion.4
  165.6 2.1 %fusion = f32[16,8,1024]{2,1,0:T(8,128)} fusion(f32[512,1024,1]{1,0,2:T(8,128)S(1)} %bitcast.60, f32[128,512]{1,0:T(8,128)S(1)} %fusion.4), kind=kOutput, calls=%fused_computation.3 | convolution fusion | flops 805306368 | bytes 2883584 | tf_op jit(solution)/shard_map/dot_general | solution.py:84
  167.7 5.8 %all-to-all-start.5 = ((f32[16,8,1024]{2,1,0:T(8,128)}), f32[16,8,1024]{2,1,0:T(8,128)S(1)}, u32[]{:S(2)}, u32[]{:S(2)}) async-start(f32[16,8,1024]{2,1,0:T(8,128)} %fusion), calls=%async_computation.5 | async-start | bytes 1048576 | tf_op jit(solution)/shard_map/all_to_all | solution.py:90
  173.5 0.8 copy.38
  174.3 16.5 %all-to-all-done.5 = f32[16,8,1024]{2,1,0:T(8,128)S(1)} async-done(((f32[16,8,1024]{2,1,0:T(8,128)}), f32[16,8,1024]{2,1,0:T(8,128)S(1)}, u32[]{:S(2)}, u32[]{:S(2)}) %all-to-all-start.5) | async-done | bytes 524320 | tf_op jit(solution)/shard_map/all_to_all | solution.py:90
  190.8 0.8 copy.45
  (7 shorter events, 0.1 us)
Async XLA Ops:
  0.6 62.5 %copy-start = (f32[512,128]{1,0:T(8,128)S(1)}, f32[512,128]{1,0:T(8,128)}, u32[]{:S(2)}) copy-start(f32[512,128]{1,0:T(8,128)} %param.6) | copy-start | bytes 786436
  167.7 23.1 %all-to-all-start.5 = ((f32[16,8,1024]{2,1,0:T(8,128)}), f32[16,8,1024]{2,1,0:T(8,128)S(1)}, u32[]{:S(2)}, u32[]{:S(2)}) async-start(f32[16,8,1024]{2,1,0:T(8,128)} %fusion), calls=%async_computation.5 | async-start | bytes 1048576 | tf_op jit(solution)/shard_map/all_to_all | solution.py:90
where the time goes:
time: 192 us
  blocking collectives  109 us (57%)
  other arithmetic  46.1 us (24%)
  waiting for transfers between devices  16.5 us (9%)
  matrix products  9.62 us (5%)
  starting transfers between devices  5.8 us (3%)
  local copies, waits for them, and re-layouts  4.05 us (2%)
    all_to_all x1, blocking collectives, shards(): lax.all_to_all(snapshots, MODE, split_axis=1, concat_axis=0, tiled=True)  60.7 us
    another operation x6, other arithmetic, orthonormal(): lower_part = jnp.linalg.cholesky(inner)  24.8 us
    all_to_all x2, blocking collectives, from_everyone(): return lax.all_to_all(copies, axis, split_axis=0, concat_axis=0, tiled=True)  21.8 us
    another operation x4, other arithmetic, orthonormal(): jax.scipy.linalg.solve_triangular(lower_part, current.T, lower=True)  21.1 us
    all_to_all x1, waiting for transfers between devices, shards(): lax.all_to_all(core_local, MODE, split_axis=0, concat_axis=1, tiled=True)  16.5 us
    all_to_all x1, blocking collectives, sum_by_axis(): lax.all_to_all(nearer, far, split_axis=0, concat_axis=0, tiled=True)  15.8 us
    all_to_all x1, blocking collectives, sent_and_summed(): parts = lax.all_to_all(cut_along(value, dim, size), axis, 0, 0, tiled=True)  10.5 us
    all_to_all x1, starting transfers between devices, shards(): lax.all_to_all(core_local, MODE, split_axis=0, concat_axis=1, tiled=True)  5.8 us
  transfers between devices with their start and end apart: 1, of which 1 were waited for; matrix products, arithmetic and copies ran while one was open for 0% of the time, Pallas kernels for 0%

commit v1 on v0

v1 whole, which is shorter than its diff:
```python
import jax
import jax.numpy as jnp
from jax import lax
from jax.experimental import pallas as pl
from jax.experimental.pallas import tpu as pltpu
from jax.sharding import Mesh
from jax.sharding import PartitionSpec as P

MODE = ("z", "core")
COLS = ("x", "y")
BLOCK = 8
LANES = 128


def spread(value):
    return jnp.broadcast_to(value, (BLOCK, LANES))


def exact_dot(left, right, dims):
    return lax.dot_general(
        left,
        right,
        (dims, ((), ())),
        precision=lax.Precision.HIGHEST,
        preferred_element_type=jnp.float32,
    )


def invert_factor(work):
    rank = work.shape[0]
    halves = (slice(0, rank), slice(rank, 2 * rank))
    for first in range(0, rank, BLOCK):
        rows = [
            [spread(work[first + i : first + i + 1, half]) for half in halves] for i in range(BLOCK)
        ]
        entry = {
            (i, j): spread(rows[i][0][:, first + j : first + j + 1])
            for i in range(BLOCK)
            for j in range(i + 1)
        }
        lower = {}
        inverse_pivot = []
        for j in range(BLOCK):
            inverse_pivot.append(lax.rsqrt(entry[j, j]))
            for i in range(j + 1, BLOCK):
                lower[i, j] = entry[i, j] * inverse_pivot[j]
            for i in range(j + 1, BLOCK):
                for m in range(i, BLOCK):
                    entry[m, i] = entry[m, i] - lower[m, j] * lower[i, j]
        solved = []
        for i in range(BLOCK):
            line = rows[i]
            for k in range(i):
                line = [part - lower[i, k] * known for part, known in zip(line, solved[k])]
            solved.append([part * inverse_pivot[i] for part in line])
            work[first + i : first + i + 1, halves[1]] = solved[i][1][:1]
        for later in range(first + BLOCK, rank, BLOCK):
            group = slice(later, later + BLOCK)
            left = work[group, halves[0]]
            right = work[group, halves[1]]
            columns = []
            for k in range(BLOCK):
                column = spread(left[:, first + k : first + k + 1])
                for m in range(k):
                    column = column - columns[m] * lower[k, m]
                columns.append(column * inverse_pivot[k])
            for k in range(BLOCK):
                left = left - columns[k] * solved[k][0]
                right = right - columns[k] * solved[k][1]
            work[group, halves[0]] = left
            work[group, halves[1]] = right


def orthonormal_kernel(projected, basis, work):
    rank = projected.shape[0]
    basis[...] = projected[...]

    def sweep(_, carry):
        current = basis[...]
        work[:, :rank] = exact_dot(current, current, ((1,), (1,)))
        across = lax.broadcasted_iota(jnp.int32, (rank, rank), 1)
        down = lax.broadcasted_iota(jnp.int32, (rank, rank), 0)
        work[:, rank:] = (across == down).astype(jnp.float32)
        invert_factor(work)
        basis[...] = exact_dot(work[:, rank:], current, ((1,), (0,)))
        return carry

    lax.fori_loop(0, 2, sweep, 0)


def orthonormal(projected):
    rank = projected.shape[0]
    return pl.pallas_call(
        orthonormal_kernel,
        out_shape=jax.ShapeDtypeStruct(projected.shape, jnp.float32),
        scratch_shapes=[pltpu.VMEM((rank, 2 * rank), jnp.float32)],
    )(projected)


def from_everyone(value, axis):
    copies = jnp.broadcast_to(value, (lax.axis_size(axis), *value.shape))
    return lax.all_to_all(copies, axis, split_axis=0, concat_axis=0, tiled=True)


def whole_sum(value):
    rows, lanes = value.shape
    tiles = value.reshape(rows // 8, 8, lanes // LANES, LANES).swapaxes(1, 2)
    halves = tiles.reshape(2, -1, 8, LANES)
    core = lax.axis_index("core")
    swap = [(0, 1), (1, 0)]
    away = lax.dynamic_index_in_dim(halves, 1 - core, 0, keepdims=False)
    kept = lax.dynamic_index_in_dim(halves, core, 0, keepdims=False)
    kept = kept + lax.ppermute(away, "core", swap)
    pieces = kept.reshape(lax.axis_size(COLS), -1, 8, LANES)
    own = lax.all_to_all(pieces, COLS, 0, 0, tiled=True).sum(axis=0)
    own = from_everyone(own, "z").sum(axis=0)
    half = from_everyone(own, COLS).reshape(kept.shape)
    other = lax.ppermute(half, "core", swap)
    first = core == 0
    joined = jnp.stack([jnp.where(first, half, other), jnp.where(first, other, half)])
    return joined.reshape(rows // 8, lanes // LANES, 8, LANES).swapaxes(1, 2).reshape(rows, lanes)


def shards(snapshots, start_basis):
    fibres = lax.all_to_all(snapshots, MODE, split_axis=1, concat_axis=0, tiled=True)
    along_cols = exact_dot(start_basis, fibres, ((0,), (0,)))
    partial_term = exact_dot(along_cols, fibres, ((1,), (1,)))
    basis = orthonormal(whole_sum(partial_term))
    core_local = exact_dot(basis, fibres, ((1,), (0,)))
    core_tensor = lax.all_to_all(core_local, MODE, split_axis=0, concat_axis=1, tiled=True)
    return (basis.T, core_tensor)


def solution(mesh):
    finer = Mesh(mesh.devices.reshape(8, 2, 4, 4), ("z", "core", "x", "y"))
    return jax.shard_map(
        shards,
        mesh=finer,
        in_specs=(P(MODE, COLS), P()),
        out_specs=(P(), P(MODE, COLS)),
        check_vma=False,
    )
```

time: 192 us -> 145 us (0.76)
  blocking collectives: 109 us -> 34.7 us
  waiting for transfers between devices: 16.5 us -> 67.4 us
  other arithmetic: 46.1 us -> 0.79 us
  starting transfers between devices: 5.8 us -> 18.4 us
  Pallas kernels: 0 us -> 10.5 us
  matrix products: 9.62 us -> 6.62 us
    all_to_all x3 -> x1, blocking collectives: 87 us -> 13.2 us  [whole_sum(): own = lax.all_to_all(pieces, COLS, 0, 0, tiled=True).sum(axis=0)]
    all_to_all x0 -> x1, waiting for transfers between devices: none -> 48.9 us  [shards(): lax.all_to_all(snapshots, MODE, split_axis=1, concat_axis=0, tiled=True)]
    another operation x10 -> x2, other arithmetic: 45.9 us -> 0.74 us  [whole_sum(): jnp.stack([jnp.where(first, half, other), jnp.where(first, other, half)])]
    pallas_call x0 -> x1, Pallas kernels: none -> 10.5 us  [orthonormal(): pl.pallas_call(orthonormal_kernel, out_shape=jax.ShapeDtypeStruct(project...]
    all_to_all x0 -> x1, starting transfers between devices: none -> 10.1 us  [shards(): lax.all_to_all(snapshots, MODE, split_axis=1, concat_axis=0, tiled=True)]
    ppermute x0 -> x2, starting transfers between devices: none -> 4.61 us  [the longest x1 4.26 us: whole_sum(): other = lax.ppermute(half, 'core', swap)]
    dot_general x5 -> x3, matrix products: 8.79 us -> 6.62 us  [exact_dot(): lax.dot_general(left, right, (dims, ((), ())), precision=lax.Precision.HI...]
    all_to_all x1, starting transfers between devices: 5.8 us -> 3.72 us  [shards(): lax.all_to_all(core_local, MODE, split_axis=0, concat_axis=1, tiled=True)]
  transfers between devices with their start and end apart: 1 -> 4, of which waited for: 1 -> 4; matrix products, arithmetic and copies ran while one was open for 0% -> 1% of each run, Pallas kernels for 0% -> 0%
where the time goes in v1:
time: 145 us; the launch traced here: 144 us
  waiting for transfers between devices  67.4 us (46%)
  blocking collectives  34.7 us (24%)
  starting transfers between devices  18.4 us (13%)
  Pallas kernels  10.5 us (7%)
  matrix products  6.62 us (5%)
  local copies, waits for them, and re-layouts  4.97 us (3%)
    all_to_all x1, waiting for transfers between devices, shards(): lax.all_to_all(snapshots, MODE, split_axis=1, concat_axis=0, tiled=True)  48.9 us
    all_to_all x2, blocking collectives, from_everyone(): return lax.all_to_all(copies, axis, split_axis=0, concat_axis=0, tiled=True)  21.4 us
    all_to_all x1, waiting for transfers between devices, shards(): lax.all_to_all(core_local, MODE, split_axis=0, concat_axis=1, tiled=True)  16.5 us
    all_to_all x1, blocking collectives, whole_sum(): own = lax.all_to_all(pieces, COLS, 0, 0, tiled=True).sum(axis=0)  13.2 us
    pallas_call x1, Pallas kernels, orthonormal(): pl.pallas_call(orthonormal_kernel, out_shape=jax.ShapeDtypeStruct(project...  10.5 us
    all_to_all x1, starting transfers between devices, shards(): lax.all_to_all(snapshots, MODE, split_axis=1, concat_axis=0, tiled=True)  10.1 us
    dot_general x3, matrix products, exact_dot(): lax.dot_general(left, right, (dims, ((), ())), precision=lax.Precision.HI...  6.62 us
    ppermute x1, starting transfers between devices, whole_sum(): other = lax.ppermute(half, 'core', swap)  4.26 us
  transfers between devices with their start and end apart: 4, of which 4 were waited for; matrix products, arithmetic and copies ran while one was open for 1% of the time, Pallas kernels for 0%

profile of v1, /device:TPU:1, one launch (start us, length us, event | category | flops | bytes accessed | tf_op | source)
XLA Modules:
  0.0 144.1 jit_solution(7836286857917466954)
XLA Ops:
  0.6 3.2 %copy.15 = f32[4,16,8,1024]{3,2,0,1:T(8,128)} copy(f32[4,16,8,1024]{3,2,1,0:T(8,128)} %bitcast.58) | data formatting | bytes 4194304 | tf_op jit(solution)/shard_map/all_to_all | solution.py:125
  3.8 0.0 copy-start.1
  3.8 10.1 %all-to-all-start = ((f32[32,16,1024]{2,0,1:T(8,128)}), f32[32,16,1024]{2,0,1:T(8,128)S(1)}, u32[]{:S(2)}, u32[]{:S(2)}) async-start(f32[32,16,1024]{2,0,1:T(8,128)} %bitcast.56), calls=%async_computation | async-start | bytes 4194304 | tf_op jit(solution)/shard_map/all_to_all | solution.py:125
  13.9 0.0 copy-done.1
  13.9 0.1 copy.9
  14.1 48.9 %all-to-all-done = f32[32,16,1024]{2,0,1:T(8,128)S(1)} async-done(((f32[32,16,1024]{2,0,1:T(8,128)}), f32[32,16,1024]{2,0,1:T(8,128)S(1)}, u32[]{:S(2)}, u32[]{:S(2)}) %all-to-all-start) | async-done | bytes 2097184 | tf_op jit(solution)/shard_map/all_to_all | solution.py:125
  63.0 1.3 convolution_bitcast_fusion
  64.2 2.2 %fusion.3 = f32[16,8,4,128]{3,1,2,0:T(8,128)S(1)} fusion(f32[16,8,1024,1]{2,1,3,0:T(8,128)S(1)} %convolution_bitcast_fusion, f32[4,128,1024,1]{2,1,0,3:T(8,128)S(1)} %bitcast.54), kind=kOutput, calls=%fused_computation.10 | convolution fusion | flops 805306368 | bytes 2883584 | tf_op jit(solution)/shard_map/dot_general | solution.py:20
  66.5 0.4 collective-permute-start
  66.9 1.1 collective-permute-done
  68.0 13.2 %all_to_all.50 = f32[16,2,8,128]{3,2,1,0:T(8,128)S(1)} all-to-all(f32[16,2,8,128]{3,2,1,0:T(8,128)S(1)} %bitcast.64), channel_id=1, replica_groups=mesh['z'=8,'core'=2,'x'=4,'y'=4] {'x','y'}, dimensions={0} | all-to-all | bytes 262144 | tf_op jit(solution)/shard_map/all_to_all | solution.py:115
  81.3 11.2 %all_to_all.51 = f32[8,2,8,128]{3,2,1,0:T(8,128)S(1)} all-to-all(f32[8,2,8,128]{3,2,1,0:T(8,128)S(1)} %broadcast_in_dim.6), channel_id=1, replica_groups=mesh['z'=8,'core'=2,'x'=4,'y'=4] {'z'}, dimensions={0} | all-to-all | bytes 131072 | tf_op jit(solution)/shard_map/all_to_all | solution.py:102
  92.5 10.2 %all_to_all.52 = f32[16,2,8,128]{3,2,1,0:T(8,128)S(1)} all-to-all(f32[16,2,8,128]{3,2,1,0:T(8,128)S(1)} %broadcast_in_dim.7), channel_id=1, replica_groups=mesh['z'=8,'core'=2,'x'=4,'y'=4] {'x','y'}, dimensions={0} | all-to-all | bytes 262144 | tf_op jit(solution)/shard_map/all_to_all | solution.py:102
  102.7 4.3 %collective-permute-start.1 = (f32[32,8,128]{2,1,0:T(8,128)S(1)}, f32[32,8,128]{2,1,0:T(8,128)S(1)}, u32[]{:S(2)}, u32[]{:S(2)}) collective-permute-start(f32[32,8,128]{2,1,0:T(8,128)S(1)} %bitcast.63), channel_id=1, source_target_pairs={{0,16},{16,0},{1,17},{17,1},{2,18},{18,2},{3,19},{19,3},{4,20},{20... | collective-permute-start | bytes 393224 | tf_op jit(solution)/shard_map/ppermute | solution.py:118
  107.0 1.0 collective-permute-done.1
  108.0 0.7 pad_maximum_fusion
  108.7 10.5 %shard_map.41 = f32[128,512]{1,0:T(8,128)} custom-call(f32[128,512]{1,0:T(8,128)} %bitcast.60), custom_call_target="tpu_custom_call" | custom-call | tf_op jit(solution)/shard_map/pallas_call | solution.py:93
  119.2 0.0 copy-start
  119.2 3.1 %fusion.1 = f32[16,8,1024]{2,1,0:T(8,128)} fusion(f32[512,1024,1]{1,0,2:T(8,128)S(1)} %bitcast.55, f32[128,512]{1,0:T(8,128)} %shard_map.41), kind=kOutput, calls=%fused_computation.4 | convolution fusion | flops 805306368 | bytes 2883584 | tf_op jit(solution)/shard_map/dot_general | solution.py:20
  122.3 3.7 %all-to-all-start.4 = ((f32[16,8,1024]{2,1,0:T(8,128)}), f32[16,8,1024]{2,1,0:T(8,128)S(1)}, u32[]{:S(2)}, u32[]{:S(2)}) async-start(f32[16,8,1024]{2,1,0:T(8,128)} %fusion.1), calls=%async_computation.4 | async-start | bytes 1048576 | tf_op jit(solution)/shard_map/all_to_all | solution.py:130
  126.0 0.0 copy-done
  126.0 0.8 copy.11
  126.8 16.5 %all-to-all-done.4 = f32[16,8,1024]{2,1,0:T(8,128)S(1)} async-done(((f32[16,8,1024]{2,1,0:T(8,128)}), f32[16,8,1024]{2,1,0:T(8,128)S(1)}, u32[]{:S(2)}, u32[]{:S(2)}) %all-to-all-start.4) | async-done | bytes 524320 | tf_op jit(solution)/shard_map/all_to_all | solution.py:130
  143.3 0.8 copy.17
  (7 shorter events, 0.1 us)
Async XLA Ops:
  3.8 10.1 %copy-start.1 = (f32[512,128]{1,0:T(8,128)S(1)}, f32[512,128]{1,0:T(8,128)}, u32[]{:S(2)}) copy-start(f32[512,128]{1,0:T(8,128)} %param.3) | copy-start | bytes 786436
  3.8 59.2 %all-to-all-start = ((f32[32,16,1024]{2,0,1:T(8,128)}), f32[32,16,1024]{2,0,1:T(8,128)S(1)}, u32[]{:S(2)}, u32[]{:S(2)}) async-start(f32[32,16,1024]{2,0,1:T(8,128)} %bitcast.56), calls=%async_computation | async-start | bytes 4194304 | tf_op jit(solution)/shard_map/all_to_all | solution.py:125
  66.5 1.4 collective-permute-start
  102.7 5.2 %collective-permute-start.1 = (f32[32,8,128]{2,1,0:T(8,128)S(1)}, f32[32,8,128]{2,1,0:T(8,128)S(1)}, u32[]{:S(2)}, u32[]{:S(2)}) collective-permute-start(f32[32,8,128]{2,1,0:T(8,128)S(1)} %bitcast.63), channel_id=1, source_target_pairs={{0,16},{16,0},{1,17},{17,1},{2,18},{18,2},{3,19},{19,3},{4,20},{20... | collective-permute-start | bytes 393224 | tf_op jit(solution)/shard_map/ppermute | solution.py:118
  119.2 6.8 %copy-start = (f32[128,512]{1,0:T(8,128)S(1)}, f32[128,512]{1,0:T(8,128)}, u32[]{:S(2)}) copy-start(f32[128,512]{1,0:T(8,128)} %shard_map.41) | copy-start | bytes 786436
  122.3 21.0 %all-to-all-start.4 = ((f32[16,8,1024]{2,1,0:T(8,128)}), f32[16,8,1024]{2,1,0:T(8,128)S(1)}, u32[]{:S(2)}, u32[]{:S(2)}) async-start(f32[16,8,1024]{2,1,0:T(8,128)} %fusion.1), calls=%async_computation.4 | async-start | bytes 1048576 | tf_op jit(solution)/shard_map/all_to_all | solution.py:130

commit v2 on v1

v2 whole, which is shorter than its diff:
```python
import jax
import jax.numpy as jnp
from jax import lax
from jax.experimental import pallas as pl
from jax.experimental.pallas import tpu as pltpu
from jax.sharding import Mesh
from jax.sharding import PartitionSpec as P

MODE = ("z", "core")
COLS = ("x", "y")
BLOCK = 8
PANEL = 64
CHUNK = 256
LANES = 128


def spread(value):
    return jnp.broadcast_to(value, (BLOCK, LANES))


def exact_dot(left, right, dims):
    return lax.dot_general(
        left,
        right,
        (dims, ((), ())),
        precision=lax.Precision.HIGHEST,
        preferred_element_type=jnp.float32,
    )


def close_dot(left, right, dims):
    return lax.dot_general(
        left,
        right,
        (dims, ((), ())),
        precision=lax.Precision.HIGH,
        preferred_element_type=jnp.float32,
    )


def two_terms(value):
    high = value.astype(jnp.bfloat16)
    return high, (value - high.astype(jnp.float32)).astype(jnp.bfloat16)


def three_products(left, right):
    left_high, left_low = left
    right_high, right_low = right
    small = jnp.dot(left_low, right_high, preferred_element_type=jnp.float32)
    small += jnp.dot(left_high, right_low, preferred_element_type=jnp.float32)
    return small + jnp.dot(left_high, right_high, preferred_element_type=jnp.float32)


def invert_factor(work, columns):
    rank = work.shape[0]
    lane = lax.broadcasted_iota(jnp.int32, (BLOCK, LANES), 1)
    for start in range(0, rank, PANEL):
        stop = start + PANEL
        for first in range(start, stop, BLOCK):
            lines = [spread(work[first + i : first + i + 1, :]) for i in range(BLOCK)]
            tile = work[first : first + BLOCK, :]
            for j in range(BLOCK):
                columns[BLOCK * j : BLOCK * (j + 1), :] = spread(tile[:, first + j : first + j + 1])
            entry = {
                (i, j): spread(columns[BLOCK * j + i : BLOCK * j + i + 1, :])
                for i in range(BLOCK)
                for j in range(i + 1)
            }
            inside = (lane >= first) & (lane < first + BLOCK)
            lines = [
                jnp.where(inside, (lane == first + i).astype(jnp.float32), line)
                for i, line in enumerate(lines)
            ]
            lower = {}
            inverse_pivot = []
            solved = []
            for j in range(BLOCK):
                inverse_pivot.append(lax.rsqrt(entry[j, j]))
                for i in range(j + 1, BLOCK):
                    lower[i, j] = entry[i, j] * inverse_pivot[j]
                for i in range(j + 1, BLOCK):
                    for m in range(i, BLOCK):
                        entry[m, i] = entry[m, i] - lower[m, j] * lower[i, j]
                solved.append(lines[j] * inverse_pivot[j])
                for i in range(j + 1, BLOCK):
                    lines[i] = lines[i] - lower[i, j] * solved[j]
                work[first + j : first + j + 1, :] = solved[j][:1]
            for later in range(first + BLOCK, stop, BLOCK):
                group = work[later : later + BLOCK, :]
                column = [spread(group[:, first + k : first + k + 1]) for k in range(BLOCK)]
                group = jnp.where(inside, 0.0, group)
                for k in range(BLOCK):
                    scaled = column[k] * inverse_pivot[k]
                    for m in range(k + 1, BLOCK):
                        column[m] = column[m] - scaled * lower[m, k]
                    group = group - scaled * solved[k]
                work[later : later + BLOCK, :] = group
        if stop < rank:
            panel = work[start:stop, :]
            across = lax.broadcasted_iota(jnp.int32, panel.shape, 1)
            down = lax.broadcasted_iota(jnp.int32, panel.shape, 0) + start
            known = jnp.where((across < stop) & (across > down), 0.0, panel)
            update = exact_dot(panel, known, ((0,), (0,)))
            rest = work[stop:, :]
            across = lax.broadcasted_iota(jnp.int32, rest.shape, 1)
            rest = jnp.where((across >= start) & (across < stop), 0.0, rest)
            work[stop:, :] = rest - update[stop:, :]


def finish_kernel(projected, fibres, basis, core, current, work, columns, whole, arrived):
    fetch = pltpu.make_async_copy(fibres, whole, arrived)
    fetch.start()
    current[...] = projected[...]

    def sweep(_, carry):
        before = current[...]
        work[...] = exact_dot(before, before, ((1,), (1,)))
        invert_factor(work, columns)
        across = lax.broadcasted_iota(jnp.int32, work.shape, 1)
        down = lax.broadcasted_iota(jnp.int32, work.shape, 0)
        inverse = jnp.where(across <= down, work[...], 0.0)
        current[...] = exact_dot(inverse, before, ((1,), (0,)))
        return carry

    lax.fori_loop(0, 2, sweep, 0)
    fetch.wait()
    rows = two_terms(current[...])
    for first in range(0, whole.shape[1], CHUNK):
        part = slice(first, first + CHUNK)
        core[:, part] = three_products(rows, two_terms(whole[:, part]))
    basis[...] = current[...].T


def finish(projected, fibres):
    rank, length = projected.shape
    some = fibres.shape[1]
    return pl.pallas_call(
        finish_kernel,
        out_shape=(
            jax.ShapeDtypeStruct((length, rank), jnp.float32),
            jax.ShapeDtypeStruct((rank, some), jnp.float32),
        ),
        in_specs=[pl.BlockSpec(memory_space=pltpu.VMEM), pl.BlockSpec(memory_space=pl.ANY)],
        scratch_shapes=[
            pltpu.VMEM((rank, length), jnp.float32),
            pltpu.VMEM((rank, rank), jnp.float32),
            pltpu.VMEM((BLOCK * BLOCK, LANES), jnp.float32),
            pltpu.VMEM(fibres.shape, jnp.float32),
            pltpu.SemaphoreType.DMA,
        ],
    )(projected, fibres)


def from_everyone(value, axis):
    copies = jnp.broadcast_to(value, (lax.axis_size(axis), *value.shape))
    return lax.all_to_all(copies, axis, split_axis=0, concat_axis=0, tiled=True)


def whole_sum(value):
    rows, lanes = value.shape
    tiles = value.reshape(rows // 8, 8, lanes // LANES, LANES).swapaxes(1, 2)
    near = ("core",) + COLS
    pieces = tiles.reshape(lax.axis_size(near), -1, 8, LANES)
    own = lax.all_to_all(pieces, near, 0, 0, tiled=True).sum(axis=0)
    own = from_everyone(own, "z").sum(axis=0)
    full = from_everyone(own, near)
    return full.reshape(rows // 8, lanes // LANES, 8, LANES).swapaxes(1, 2).reshape(rows, lanes)


def shards(snapshots, start_basis):
    fibres = lax.all_to_all(snapshots, MODE, split_axis=1, concat_axis=0, tiled=True)
    along_cols = close_dot(start_basis, fibres, ((0,), (0,)))
    partial_term = close_dot(along_cols, fibres, ((1,), (1,)))
    basis, core_local = finish(whole_sum(partial_term), fibres)
    core_tensor = lax.all_to_all(core_local, MODE, split_axis=0, concat_axis=1, tiled=True)
    return (basis, core_tensor)


def solution(mesh):
    finer = Mesh(mesh.devices.reshape(8, 2, 4, 4), ("z", "core", "x", "y"))
    return jax.shard_map(
        shards,
        mesh=finer,
        in_specs=(P(MODE, COLS), P()),
        out_specs=(P(), P(MODE, COLS)),
        check_vma=False,
    )
```

time: 145 us -> 140 us (0.966)
  blocking collectives: 34.7 us -> 63 us
  waiting for transfers between devices: 67.4 us -> 48.9 us
  starting transfers between devices: 18.4 us -> 10.1 us
  matrix products: 6.62 us -> 1.93 us
    all_to_all x1 -> x2, blocking collectives: 13.2 us -> 37.3 us  [the longest x1 21.3 us: shards(): lax.all_to_all(core_local, MODE, split_axis=0, concat_axis=1, tiled=True)]
    all_to_all x1 -> x0, waiting for transfers between devices: 16.5 us -> none  [shards(): lax.all_to_all(core_local, MODE, split_axis=0, concat_axis=1, tiled=True)]
    dot_general x3 -> x2, matrix products: 6.62 us -> 1.93 us  [close_dot(): lax.dot_general(left, right, (dims, ((), ())), precision=lax.Precision.HI...]
    ppermute x2 -> x0, starting transfers between devices: 4.61 us -> none  [the longest x1 4.26 us: whole_sum(): other = lax.ppermute(half, 'core', swap)]
    all_to_all x2, blocking collectives: 21.4 us -> 25.6 us  [from_everyone(): return lax.all_to_all(copies, axis, split_axis=0, concat_axis=0, tiled=True)]
    all_to_all x1 -> x0, starting transfers between devices: 3.72 us -> none  [shards(): lax.all_to_all(core_local, MODE, split_axis=0, concat_axis=1, tiled=True)]
    ppermute x2 -> x0, waiting for transfers between devices: 2.06 us -> none  [the longest x1 1.08 us: whole_sum(): kept = kept + lax.ppermute(away, 'core', swap)]
  transfers between devices with their start and end apart: 4 -> 1, of which waited for: 4 -> 1; matrix products, arithmetic and copies ran while one was open for 1% -> 0% of each run, Pallas kernels for 0% -> 0%
where the time goes in v2:
time: 140 us; the launch traced here: 139 us
  blocking collectives  63 us (45%)
  waiting for transfers between devices  48.9 us (35%)
  Pallas kernels  10.5 us (8%)
  starting transfers between devices  10.1 us (7%)
  local copies, waits for them, and re-layouts  4.15 us (3%)
  matrix products  1.93 us (1%)
    all_to_all x1, waiting for transfers between devices, shards(): lax.all_to_all(snapshots, MODE, split_axis=1, concat_axis=0, tiled=True)  48.9 us
    all_to_all x2, blocking collectives, from_everyone(): return lax.all_to_all(copies, axis, split_axis=0, concat_axis=0, tiled=True)  25.6 us
    all_to_all x1, blocking collectives, shards(): lax.all_to_all(core_local, MODE, split_axis=0, concat_axis=1, tiled=True)  21.3 us
    all_to_all x1, blocking collectives, whole_sum(): own = lax.all_to_all(pieces, near, 0, 0, tiled=True).sum(axis=0)  16 us
    pallas_call x1, Pallas kernels, finish(): pl.pallas_call(finish_kernel, out_shape=(jax.ShapeDtypeStruct((length, ra...  10.5 us
    all_to_all x1, starting transfers between devices, shards(): lax.all_to_all(snapshots, MODE, split_axis=1, concat_axis=0, tiled=True)  10.1 us
    all_to_all x1, local copies, waits for them, and re-layouts, shards(): lax.all_to_all(snapshots, MODE, split_axis=1, concat_axis=0, tiled=True)  3.19 us
  transfers between devices with their start and end apart: 1, of which 1 were waited for; matrix products, arithmetic and copies ran while one was open for 0% of the time, Pallas kernels for 0%

profile of v2, /device:TPU:1, one launch (start us, length us, event | category | flops | bytes accessed | tf_op | source)
XLA Modules:
  0.0 139.3 jit_solution(16087751923492885710)
XLA Ops:
  0.6 3.2 %copy.12 = f32[4,16,8,1024]{3,2,0,1:T(8,128)} copy(f32[4,16,8,1024]{3,2,1,0:T(8,128)} %bitcast.41) | data formatting | bytes 4194304 | tf_op jit(solution)/shard_map/all_to_all | solution.py:171
  3.8 0.0 copy-start.1
  3.8 10.1 %all-to-all-start = ((f32[32,16,1024]{2,0,1:T(8,128)}), f32[32,16,1024]{2,0,1:T(8,128)S(1)}, u32[]{:S(2)}, u32[]{:S(2)}) async-start(f32[32,16,1024]{2,0,1:T(8,128)} %bitcast.40), calls=%async_computation | async-start | bytes 4194304 | tf_op jit(solution)/shard_map/all_to_all | solution.py:171
  13.9 0.0 copy-done.1
  13.9 0.1 copy.7
  14.1 48.9 %all-to-all-done = f32[32,16,1024]{2,0,1:T(8,128)S(1)} async-done(((f32[32,16,1024]{2,0,1:T(8,128)}), f32[32,16,1024]{2,0,1:T(8,128)S(1)}, u32[]{:S(2)}, u32[]{:S(2)}) %all-to-all-start) | async-done | bytes 2097184 | tf_op jit(solution)/shard_map/all_to_all | solution.py:171
  63.0 0.0 copy-start
  63.0 0.8 convolution_bitcast_fusion
  63.7 1.2 fusion.1
  64.9 0.0 copy-done
  64.9 16.0 %all_to_all.53 = f32[32,2,8,128]{3,2,1,0:T(8,128)S(1)} all-to-all(f32[32,2,8,128]{3,2,1,0:T(8,128)S(1)} %bitcast.44), channel_id=1, replica_groups=mesh['z'=8,'core'=2,'x'=4,'y'=4] {'core','x','y'}, dimensions={0} | all-to-all | bytes 524288 | tf_op jit(solution)/shard_map/all_to_all | solution.py:164
  81.0 11.4 %all_to_all.54 = f32[8,2,8,128]{3,2,1,0:T(8,128)S(1)} all-to-all(f32[8,2,8,128]{3,2,1,0:T(8,128)S(1)} %broadcast_in_dim.6), channel_id=1, replica_groups=mesh['z'=8,'core'=2,'x'=4,'y'=4] {'z'}, dimensions={0} | all-to-all | bytes 131072 | tf_op jit(solution)/shard_map/all_to_all | solution.py:156
  92.4 14.3 %all_to_all.55 = f32[32,2,8,128]{3,2,1,0:T(8,128)} all-to-all(f32[32,2,8,128]{3,2,1,0:T(8,128)S(1)} %broadcast_in_dim.7), channel_id=1, replica_groups=mesh['z'=8,'core'=2,'x'=4,'y'=4] {'core','x','y'}, dimensions={0} | all-to-all | bytes 524288 | tf_op jit(solution)/shard_map/all_to_all | solution.py:156
  106.7 10.5 %shard_map.41 = (f32[512,128]{1,0:T(8,128)}, f32[128,1024]{1,0:T(8,128)}) custom-call(f32[128,512]{1,0:T(8,128)} %bitcast.43, f32[512,1024]{1,0:T(8,128)} %bitcast.39), custom_call_target="tpu_custom_call" | custom-call | tf_op jit(solution)/shard_map/pallas_call | solution.py:137
  117.1 21.3 %all_to_all.56 = f32[16,8,1024]{2,1,0:T(8,128)S(1)} all-to-all(f32[16,8,1024]{2,1,0:T(8,128)} %bitcast.45), channel_id=1, replica_groups=mesh['z'=8,'core'=2,'x'=4,'y'=4] {'z','core'}, dimensions={0} | all-to-all | bytes 1048576 | tf_op jit(solution)/shard_map/all_to_all | solution.py:175
  138.5 0.8 copy.14
  (4 shorter events, 0.1 us)
Async XLA Ops:
  3.8 10.1 %copy-start.1 = (f32[512,128]{1,0:T(8,128)S(1)}, f32[512,128]{1,0:T(8,128)}, u32[]{:S(2)}) copy-start(f32[512,128]{1,0:T(8,128)} %param.3) | copy-start | bytes 786436
  3.8 59.2 %all-to-all-start = ((f32[32,16,1024]{2,0,1:T(8,128)}), f32[32,16,1024]{2,0,1:T(8,128)S(1)}, u32[]{:S(2)}, u32[]{:S(2)}) async-start(f32[32,16,1024]{2,0,1:T(8,128)} %bitcast.40), calls=%async_computation | async-start | bytes 4194304 | tf_op jit(solution)/shard_map/all_to_all | solution.py:171
  63.0 2.0 %copy-start = (f32[32,16,1024]{2,0,1:T(8,128)}, f32[32,16,1024]{2,0,1:T(8,128)S(1)}, u32[]{:S(2)}) copy-start(f32[32,16,1024]{2,0,1:T(8,128)S(1)} %all-to-all-done) | copy-start | bytes 6291460

commit v3 on v2

--- a/solution.py
+++ b/solution.py
@@ -43,12 +43,14 @@
     return high, (value - high.astype(jnp.float32)).astype(jnp.bfloat16)
 
 
-def three_products(left, right):
+def three_products(left, right, dims=((1,), (0,))):
+    def product(one, other):
+        return lax.dot_general(one, other, (dims, ((), ())), preferred_element_type=jnp.float32)
+
     left_high, left_low = left
     right_high, right_low = right
-    small = jnp.dot(left_low, right_high, preferred_element_type=jnp.float32)
-    small += jnp.dot(left_high, right_low, preferred_element_type=jnp.float32)
-    return small + jnp.dot(left_high, right_high, preferred_element_type=jnp.float32)
+    small = product(left_low, right_high) + product(left_high, right_low)
+    return small + product(left_high, right_high)
 
 
 def invert_factor(work, columns):
@@ -100,21 +102,23 @@
             across = lax.broadcasted_iota(jnp.int32, panel.shape, 1)
             down = lax.broadcasted_iota(jnp.int32, panel.shape, 0) + start
             known = jnp.where((across < stop) & (across > down), 0.0, panel)
-            update = exact_dot(panel, known, ((0,), (0,)))
+            update = three_products(two_terms(panel), two_terms(known), ((0,), (0,)))
             rest = work[stop:, :]
             across = lax.broadcasted_iota(jnp.int32, rest.shape, 1)
             rest = jnp.where((across >= start) & (across < stop), 0.0, rest)
             work[stop:, :] = rest - update[stop:, :]
 
 
-def finish_kernel(projected, fibres, basis, core, current, work, columns, whole, arrived):
-    fetch = pltpu.make_async_copy(fibres, whole, arrived)
-    fetch.start()
-    current[...] = projected[...]
+def finish_kernel(place, own, other, fibres, basis, core, current, work, columns):
+    rows = own.shape[0]
+    first = place[0] == 0
+    current[:rows, :] = jnp.where(first, own[...], other[...])
+    current[rows:, :] = jnp.where(first, other[...], own[...])
 
     def sweep(_, carry):
         before = current[...]
-        work[...] = exact_dot(before, before, ((1,), (1,)))
+        terms = two_terms(before)
+        work[...] = three_products(terms, terms, ((1,), (1,)))
         invert_factor(work, columns)
         across = lax.broadcasted_iota(jnp.int32, work.shape, 1)
         down = lax.broadcasted_iota(jnp.int32, work.shape, 0)
@@ -123,32 +127,67 @@
         return carry
 
     lax.fori_loop(0, 2, sweep, 0)
-    fetch.wait()
     rows = two_terms(current[...])
-    for first in range(0, whole.shape[1], CHUNK):
+    for first in range(0, fibres.shape[1], CHUNK):
         part = slice(first, first + CHUNK)
-        core[:, part] = three_products(rows, two_terms(whole[:, part]))
+        core[:, part] = three_products(rows, two_terms(fibres[:, part]))
     basis[...] = current[...].T
 
 
-def finish(projected, fibres):
-    rank, length = projected.shape
+def in_vmem(value):
+    return pltpu.with_memory_space_constraint(value, pltpu.VMEM)
+
+
+def finish(core, own, other, fibres):
+    rank, length = own.shape[0] * 2, own.shape[1]
     some = fibres.shape[1]
     return pl.pallas_call(
         finish_kernel,
         out_shape=(
             jax.ShapeDtypeStruct((length, rank), jnp.float32),
-            jax.ShapeDtypeStruct((rank, some), jnp.float32),
+            pltpu.VMEM((rank, some), jnp.float32),
         ),
-        in_specs=[pl.BlockSpec(memory_space=pltpu.VMEM), pl.BlockSpec(memory_space=pl.ANY)],
+        in_specs=[
+            pl.BlockSpec(memory_space=pltpu.SMEM),
+            pl.BlockSpec(memory_space=pltpu.VMEM),
+            pl.BlockSpec(memory_space=pltpu.VMEM),
+            pl.BlockSpec(memory_space=pltpu.VMEM),
+        ],
+        out_specs=(pl.BlockSpec(memory_space=pltpu.VMEM), pl.BlockSpec(memory_space=pltpu.VMEM)),
         scratch_shapes=[
             pltpu.VMEM((rank, length), jnp.float32),
             pltpu.VMEM((rank, rank), jnp.float32),
             pltpu.VMEM((BLOCK * BLOCK, LANES), jnp.float32),
-            pltpu.VMEM(fibres.shape, jnp.float32),
-            pltpu.SemaphoreType.DMA,
         ],
-    )(projected, fibres)
+        compiler_params=pltpu.CompilerParams(vmem_limit_bytes=16 * 2**20),
+    )(
+        core[None], in_vmem(own), in_vmem(other), in_vmem(fibres)
+    )
+
+
+def regroup_kernel(snapshots, pieces, arrived):
+    members, _, some = pieces.shape
+    arrivals = []
+    for member in range(members):
+        columns = slice(member * some, (member + 1) * some)
+        arrivals.append(
+            pltpu.make_async_copy(snapshots.at[:, columns], pieces.at[member], arrived.at[member])
+        )
+        arrivals[-1].start()
+    for arrival in arrivals:
+        arrival.wait()
+
+
+def regroup(snapshots, members):
+    rows, length = snapshots.shape
+    return pl.pallas_call(
+        regroup_kernel,
+        out_shape=pltpu.VMEM((members, rows, length // members), jnp.float32),
+        in_specs=[pl.BlockSpec(memory_space=pl.ANY)],
+        out_specs=pl.BlockSpec(memory_space=pltpu.VMEM),
+        scratch_shapes=[pltpu.SemaphoreType.DMA((members,))],
+        compiler_params=pltpu.CompilerParams(vmem_limit_bytes=4 * 2**20),
+    )(pltpu.with_memory_space_constraint(snapshots, pltpu.HBM))
 
 
 def from_everyone(value, axis):
@@ -156,22 +195,35 @@
     return lax.all_to_all(copies, axis, split_axis=0, concat_axis=0, tiled=True)
 
 
-def whole_sum(value):
+def half_sums(value, core):
     rows, lanes = value.shape
     tiles = value.reshape(rows // 8, 8, lanes // LANES, LANES).swapaxes(1, 2)
-    near = ("core",) + COLS
-    pieces = tiles.reshape(lax.axis_size(near), -1, 8, LANES)
-    own = lax.all_to_all(pieces, near, 0, 0, tiled=True).sum(axis=0)
+    halves = tiles.reshape(2, -1, 8, LANES)
+    swap = [(0, 1), (1, 0)]
+    away = lax.dynamic_index_in_dim(halves, 1 - core, 0, keepdims=False)
+    kept = lax.dynamic_index_in_dim(halves, core, 0, keepdims=False)
+    kept = kept + lax.ppermute(away, "core", swap)
+    pieces = kept.reshape(lax.axis_size(COLS), -1, 8, LANES)
+    own = lax.all_to_all(pieces, COLS, 0, 0, tiled=True).sum(axis=0)
     own = from_everyone(own, "z").sum(axis=0)
-    full = from_everyone(own, near)
-    return full.reshape(rows // 8, lanes // LANES, 8, LANES).swapaxes(1, 2).reshape(rows, lanes)
+    half = from_everyone(own, COLS)
+    other = lax.ppermute(half, "core", swap)
+    shape = (rows // 16, lanes // LANES, 8, LANES)
+    return [
+        part.reshape(shape).swapaxes(1, 2).reshape(rows // 2, lanes) for part in (half, other)
+    ]
 
 
 def shards(snapshots, start_basis):
-    fibres = lax.all_to_all(snapshots, MODE, split_axis=1, concat_axis=0, tiled=True)
+    pieces = regroup(snapshots, lax.axis_size(MODE))
+    core = lax.axis_index("core")
+    pieces, core = lax.optimization_barrier((pieces, core))
+    fibres = lax.all_to_all(pieces, MODE, 0, 0, tiled=True)
+    fibres = fibres.reshape(-1, fibres.shape[-1])
+    fibres, start_basis, core = lax.optimization_barrier((fibres, start_basis, core))
     along_cols = close_dot(start_basis, fibres, ((0,), (0,)))
     partial_term = close_dot(along_cols, fibres, ((1,), (1,)))
-    basis, core_local = finish(whole_sum(partial_term), fibres)
+    basis, core_local = finish(core, *half_sums(partial_term, core), fibres)
     core_tensor = lax.all_to_all(core_local, MODE, split_axis=0, concat_axis=1, tiled=True)
     return (basis, core_tensor)
 

time: 140 us -> 134 us (0.957)
  blocking collectives: 63 us -> 114 us
  waiting for transfers between devices: 48.9 us -> 2.32 us
  starting transfers between devices: 10.1 us -> 4.21 us
  local copies, waits for them, and re-layouts: 4.15 us -> 0.84 us
    all_to_all x1 -> x2, blocking collectives: 16 us -> 74 us  [the longest x1 60.7 us: shards(): fibres = lax.all_to_all(pieces, MODE, 0, 0, tiled=True)]
    all_to_all x1 -> x0, waiting for transfers between devices: 48.9 us -> none  [shards(): lax.all_to_all(snapshots, MODE, split_axis=1, concat_axis=0, tiled=True)]
    all_to_all x1 -> x0, starting transfers between devices: 10.1 us -> none  [shards(): lax.all_to_all(snapshots, MODE, split_axis=1, concat_axis=0, tiled=True)]
    all_to_all x2, blocking collectives: 25.6 us -> 19.6 us  [from_everyone(): return lax.all_to_all(copies, axis, split_axis=0, concat_axis=0, tiled=True)]
    ppermute x0 -> x2, starting transfers between devices: none -> 4.21 us  [the longest x1 4.11 us: half_sums(): other = lax.ppermute(half, 'core', swap)]
    all_to_all x1 -> x0, local copies, waits for them, and re-layouts: 3.19 us -> none  [shards(): lax.all_to_all(snapshots, MODE, split_axis=1, concat_axis=0, tiled=True)]
    ppermute x0 -> x2, waiting for transfers between devices: none -> 2.32 us  [the longest x1 1.33 us: half_sums(): kept = kept + lax.ppermute(away, 'core', swap)]
    pallas_call x1, Pallas kernels: 10.5 us -> 8.38 us  [finish(): pl.pallas_call(finish_kernel, out_shape=(jax.ShapeDtypeStruct((length, ra...]
  transfers between devices with their start and end apart: 1 -> 2, of which waited for: 1 -> 2; matrix products, arithmetic and copies ran while one was open for 0% -> 0% of each run, Pallas kernels for 0% -> 0%
where the time goes in v3:
time: 134 us
  blocking collectives  114 us (85%)
  Pallas kernels  10.2 us (8%)
  starting transfers between devices  4.21 us (3%)
  waiting for transfers between devices  2.32 us (2%)
  matrix products  1.91 us (1%)
    all_to_all x1, blocking collectives, shards(): fibres = lax.all_to_all(pieces, MODE, 0, 0, tiled=True)  60.7 us
    all_to_all x1, blocking collectives, shards(): lax.all_to_all(core_local, MODE, split_axis=0, concat_axis=1, tiled=True)  20.1 us
    all_to_all x2, blocking collectives, from_everyone(): return lax.all_to_all(copies, axis, split_axis=0, concat_axis=0, tiled=True)  19.6 us
    all_to_all x1, blocking collectives, half_sums(): own = lax.all_to_all(pieces, COLS, 0, 0, tiled=True).sum(axis=0)  13.3 us
    pallas_call x1, Pallas kernels, finish(): pl.pallas_call(finish_kernel, out_shape=(jax.ShapeDtypeStruct((length, ra...  8.38 us
    ppermute x1, starting transfers between devices, half_sums(): other = lax.ppermute(half, 'core', swap)  4.11 us
  transfers between devices with their start and end apart: 2, of which 2 were waited for; matrix products, arithmetic and copies ran while one was open for 0% of the time, Pallas kernels for 0%

profile of v3, /device:TPU:1, one launch (start us, length us, event | category | flops | bytes accessed | tf_op | source)
XLA Modules:
  0.0 133.9 jit_solution(1509593571735468149)
XLA Ops:
  0.6 0.0 copy-start
  0.6 1.8 %shard_map.41 = f32[16,32,1024]{2,1,0:T(8,128)S(1)} custom-call(f32[32,16384]{1,0:T(8,128)} %snapshots.1), custom_call_target="tpu_custom_call" | custom-call | tf_op jit(solution)/shard_map/pallas_call | solution.py:183
  2.4 60.7 %all_to_all.39 = f32[16,32,1024]{2,1,0:T(8,128)S(1)} all-to-all(f32[16,32,1024]{2,1,0:T(8,128)S(1)} %shard_map.41), channel_id=1, replica_groups=mesh['z'=8,'core'=2,'x'=4,'y'=4] {'z','core'}, dimensions={0} | all-to-all | bytes 4194304 | tf_op jit(solution)/shard_map/all_to_all | solution.py:221
  63.1 0.0 copy-done
  63.1 0.7 fusion
  63.8 1.2 fusion.1
  65.1 0.1 collective-permute-start
  65.2 1.3 collective-permute-done
  66.5 13.3 %all_to_all.40 = f32[16,2,8,128]{3,2,1,0:T(8,128)S(1)} all-to-all(f32[16,2,8,128]{3,2,1,0:T(8,128)S(1)} %bitcast.39), channel_id=1, replica_groups=mesh['z'=8,'core'=2,'x'=4,'y'=4] {'x','y'}, dimensions={0} | all-to-all | bytes 262144 | tf_op jit(solution)/shard_map/all_to_all | solution.py:207
  79.9 9.7 %all_to_all.41 = f32[8,2,8,128]{3,2,1,0:T(8,128)S(1)} all-to-all(f32[8,2,8,128]{3,2,1,0:T(8,128)S(1)} %broadcast_in_dim.10), channel_id=1, replica_groups=mesh['z'=8,'core'=2,'x'=4,'y'=4] {'z'}, dimensions={0} | all-to-all | bytes 131072 | tf_op jit(solution)/shard_map/all_to_all | solution.py:195
  89.6 9.9 %all_to_all.42 = f32[16,2,8,128]{3,2,1,0:T(8,128)S(1)} all-to-all(f32[16,2,8,128]{3,2,1,0:T(8,128)S(1)} %broadcast_in_dim.11), channel_id=1, replica_groups=mesh['z'=8,'core'=2,'x'=4,'y'=4] {'x','y'}, dimensions={0} | all-to-all | bytes 262144 | tf_op jit(solution)/shard_map/all_to_all | solution.py:195
  99.5 4.1 %collective-permute-start.1 = (f32[16,2,8,128]{3,2,1,0:T(8,128)S(1)}, f32[16,2,8,128]{3,2,1,0:T(8,128)S(1)}, u32[]{:S(2)}, u32[]{:S(2)}) collective-permute-start(f32[16,2,8,128]{3,2,1,0:T(8,128)S(1)} %all_to_all.42), channel_id=1, source_target_pairs={{0,16},{16,0},{1,17},{17,1},{2,18},{18,2},{3,19},{19,3},{4,20},{20... | collective-permute-start | bytes 393224 | tf_op jit(solution)/shard_map/ppermute | solution.py:210
  103.7 1.0 collective-permute-done.1
  104.6 8.4 %shard_map.42 = (f32[512,128]{1,0:T(8,128)}, f32[128,1024]{1,0:T(8,128)S(1)}) custom-call(s32[1]{0:T(128)} %bitcast.1.place, f32[64,512]{1,0:T(8,128)S(1)} %bitcast.33, f32[64,512]{1,0:T(8,128)S(1)} %bitcast.35, f32[512,1024]{1,0:T(8,128)S(1)} %bitcast.32), custom_call_target="tpu_custom_call" | custom-call | tf_op jit(solution)/shard_map/pallas_call | solution.py:144
  113.0 20.1 %all_to_all.43 = f32[16,8,1024]{2,1,0:T(8,128)S(1)} all-to-all(f32[16,8,1024]{2,1,0:T(8,128)S(1)} %bitcast.34), channel_id=1, replica_groups=mesh['z'=8,'core'=2,'x'=4,'y'=4] {'z','core'}, dimensions={0} | all-to-all | bytes 1048576 | tf_op jit(solution)/shard_map/all_to_all | solution.py:227
  133.1 0.8 copy.5
  (6 shorter events, 0.1 us)
Async XLA Ops:
  0.6 62.5 %copy-start = (f32[512,128]{1,0:T(8,128)S(1)}, f32[512,128]{1,0:T(8,128)}, u32[]{:S(2)}) copy-start(f32[512,128]{1,0:T(8,128)} %param.3) | copy-start | bytes 786436
  65.1 1.4 %collective-permute-start = (f32[32,8,128]{2,1,0:T(8,128)S(1)}, f32[32,8,128]{2,1,0:T(8,128)S(1)}, u32[]{:S(2)}, u32[]{:S(2)}) collective-permute-start(f32[32,8,128]{2,1,0:T(8,128)S(1)} %dynamic-slice_bitcast_fusion), channel_id=1, source_target_pairs={{0,16},{16,0},{1,17},{17,1},{2,18},{18,2},{3,19},{19,3},{4,20},{20... | collective-permute-start | bytes 393224 | tf_op jit(solution)/shard_map/ppermute | solution.py:205
  99.5 5.1 %collective-permute-start.1 = (f32[16,2,8,128]{3,2,1,0:T(8,128)S(1)}, f32[16,2,8,128]{3,2,1,0:T(8,128)S(1)}, u32[]{:S(2)}, u32[]{:S(2)}) collective-permute-start(f32[16,2,8,128]{3,2,1,0:T(8,128)S(1)} %all_to_all.42), channel_id=1, source_target_pairs={{0,16},{16,0},{1,17},{17,1},{2,18},{18,2},{3,19},{19,3},{4,20},{20... | collective-permute-start | bytes 393224 | tf_op jit(solution)/shard_map/ppermute | solution.py:210

commit v4 on v3

--- a/solution.py
+++ b/solution.py
@@ -76,17 +76,25 @@
             lower = {}
             inverse_pivot = []
             solved = []
-            for j in range(BLOCK):
+            for j in range(0, BLOCK, 2):
+                determinant = entry[j, j] * entry[j + 1, j + 1] - entry[j + 1, j] * entry[j + 1, j]
                 inverse_pivot.append(lax.rsqrt(entry[j, j]))
-                for i in range(j + 1, BLOCK):
+                root = entry[j, j] * inverse_pivot[j]
+                inverse_pivot.append(lax.rsqrt(determinant) * root)
+                lower[j + 1, j] = entry[j + 1, j] * inverse_pivot[j]
+                for i in range(j + 2, BLOCK):
                     lower[i, j] = entry[i, j] * inverse_pivot[j]
-                for i in range(j + 1, BLOCK):
+                    rest = entry[i, j + 1] - lower[i, j] * lower[j + 1, j]
+                    lower[i, j + 1] = rest * inverse_pivot[j + 1]
+                for i in range(j + 2, BLOCK):
                     for m in range(i, BLOCK):
-                        entry[m, i] = entry[m, i] - lower[m, j] * lower[i, j]
-                solved.append(lines[j] * inverse_pivot[j])
-                for i in range(j + 1, BLOCK):
-                    lines[i] = lines[i] - lower[i, j] * solved[j]
-                work[first + j : first + j + 1, :] = solved[j][:1]
+                        for k in (j, j + 1):
+                            entry[m, i] = entry[m, i] - lower[m, k] * lower[i, k]
+                for k in (j, j + 1):
+                    solved.append(lines[k] * inverse_pivot[k])
+                    for i in range(k + 1, BLOCK):
+                        lines[i] = lines[i] - lower[i, k] * solved[k]
+                    work[first + k : first + k + 1, :] = solved[k][:1]
             for later in range(first + BLOCK, stop, BLOCK):
                 group = work[later : later + BLOCK, :]
                 column = [spread(group[:, first + k : first + k + 1]) for k in range(BLOCK)]
@@ -109,11 +117,16 @@
             work[stop:, :] = rest - update[stop:, :]
 
 
-def finish_kernel(place, own, other, fibres, basis, core, current, work, columns):
+def finish_kernel(
+    place, own, other, fibres, basis, core, current, work, columns, turned, left
+):
     rows = own.shape[0]
     first = place[0] == 0
     current[:rows, :] = jnp.where(first, own[...], other[...])
     current[rows:, :] = jnp.where(first, other[...], own[...])
+    for top in range(0, current.shape[0], BLOCK):
+        some = current[top : top + BLOCK, :]
+        current[top : top + BLOCK, :] = some * lax.rsqrt(jnp.sum(some * some, axis=1, keepdims=True))
 
     def sweep(_, carry):
         before = current[...]
@@ -127,11 +140,14 @@
         return carry
 
     lax.fori_loop(0, 2, sweep, 0)
+    turned[...] = current[...].T
+    send = pltpu.make_async_copy(turned, basis, left)
+    send.start()
     rows = two_terms(current[...])
     for first in range(0, fibres.shape[1], CHUNK):
         part = slice(first, first + CHUNK)
         core[:, part] = three_products(rows, two_terms(fibres[:, part]))
-    basis[...] = current[...].T
+    send.wait()
 
 
 def in_vmem(value):
@@ -144,7 +160,7 @@
     return pl.pallas_call(
         finish_kernel,
         out_shape=(
-            jax.ShapeDtypeStruct((length, rank), jnp.float32),
+            pltpu.HBM((length, rank), jnp.float32),
             pltpu.VMEM((rank, some), jnp.float32),
         ),
         in_specs=[
@@ -153,11 +169,13 @@
             pl.BlockSpec(memory_space=pltpu.VMEM),
             pl.BlockSpec(memory_space=pltpu.VMEM),
         ],
-        out_specs=(pl.BlockSpec(memory_space=pltpu.VMEM), pl.BlockSpec(memory_space=pltpu.VMEM)),
+        out_specs=(pl.BlockSpec(memory_space=pl.ANY), pl.BlockSpec(memory_space=pltpu.VMEM)),
         scratch_shapes=[
             pltpu.VMEM((rank, length), jnp.float32),
             pltpu.VMEM((rank, rank), jnp.float32),
             pltpu.VMEM((BLOCK * BLOCK, LANES), jnp.float32),
+            pltpu.VMEM((length, rank), jnp.float32),
+            pltpu.SemaphoreType.DMA,
         ],
         compiler_params=pltpu.CompilerParams(vmem_limit_bytes=16 * 2**20),
     )(

time: 134 us -> 134 us (level)
  no operation moved by 1% of the time
where the time goes in v4:
time: 134 us; the launch traced here: 133 us
  blocking collectives  114 us (85%)
  Pallas kernels  9.52 us (7%)
  starting transfers between devices  4.21 us (3%)
  waiting for transfers between devices  2.32 us (2%)
  matrix products  1.91 us (1%)
    all_to_all x1, blocking collectives, shards(): fibres = lax.all_to_all(pieces, MODE, 0, 0, tiled=True)  60.7 us
    all_to_all x1, blocking collectives, shards(): lax.all_to_all(core_local, MODE, split_axis=0, concat_axis=1, tiled=True)  20.1 us
    all_to_all x2, blocking collectives, from_everyone(): return lax.all_to_all(copies, axis, split_axis=0, concat_axis=0, tiled=True)  19.6 us
    all_to_all x1, blocking collectives, half_sums(): own = lax.all_to_all(pieces, COLS, 0, 0, tiled=True).sum(axis=0)  13.3 us
    pallas_call x1, Pallas kernels, finish(): pl.pallas_call(finish_kernel, out_shape=(pltpu.HBM((length, rank), jnp.fl...  7.75 us
    ppermute x1, starting transfers between devices, half_sums(): other = lax.ppermute(half, 'core', swap)  4.11 us
  transfers between devices with their start and end apart: 2, of which 2 were waited for; matrix products, arithmetic and copies ran while one was open for 0% of the time, Pallas kernels for 0%

profile of v4, /device:TPU:1, one launch (start us, length us, event | category | flops | bytes accessed | tf_op | source)
XLA Modules:
  0.0 133.3 jit_solution(2988684872071489439)
XLA Ops:
  0.6 0.0 copy-start
  0.6 1.8 %shard_map.41 = f32[16,32,1024]{2,1,0:T(8,128)S(1)} custom-call(f32[32,16384]{1,0:T(8,128)} %snapshots.1), custom_call_target="tpu_custom_call" | custom-call | tf_op jit(solution)/shard_map/pallas_call | solution.py:201
  2.4 60.7 %all_to_all.39 = f32[16,32,1024]{2,1,0:T(8,128)S(1)} all-to-all(f32[16,32,1024]{2,1,0:T(8,128)S(1)} %shard_map.41), channel_id=1, replica_groups=mesh['z'=8,'core'=2,'x'=4,'y'=4] {'z','core'}, dimensions={0} | all-to-all | bytes 4194304 | tf_op jit(solution)/shard_map/all_to_all | solution.py:239
  63.1 0.0 copy-done
  63.1 0.7 fusion
  63.8 1.2 fusion.1
  65.1 0.1 collective-permute-start
  65.2 1.3 %collective-permute-done = f32[32,8,128]{2,1,0:T(8,128)S(1)} collective-permute-done((f32[32,8,128]{2,1,0:T(8,128)S(1)}, f32[32,8,128]{2,1,0:T(8,128)S(1)}, u32[]{:S(2)}, u32[]{:S(2)}) %collective-permute-start) | collective-permute-done | bytes 131104 | tf_op jit(solution)/shard_map/ppermute | solution.py:223
  66.5 13.3 %all_to_all.40 = f32[16,2,8,128]{3,2,1,0:T(8,128)S(1)} all-to-all(f32[16,2,8,128]{3,2,1,0:T(8,128)S(1)} %bitcast.39), channel_id=1, replica_groups=mesh['z'=8,'core'=2,'x'=4,'y'=4] {'x','y'}, dimensions={0} | all-to-all | bytes 262144 | tf_op jit(solution)/shard_map/all_to_all | solution.py:225
  79.9 9.7 %all_to_all.41 = f32[8,2,8,128]{3,2,1,0:T(8,128)S(1)} all-to-all(f32[8,2,8,128]{3,2,1,0:T(8,128)S(1)} %broadcast_in_dim.10), channel_id=1, replica_groups=mesh['z'=8,'core'=2,'x'=4,'y'=4] {'z'}, dimensions={0} | all-to-all | bytes 131072 | tf_op jit(solution)/shard_map/all_to_all | solution.py:213
  89.6 9.9 %all_to_all.42 = f32[16,2,8,128]{3,2,1,0:T(8,128)S(1)} all-to-all(f32[16,2,8,128]{3,2,1,0:T(8,128)S(1)} %broadcast_in_dim.11), channel_id=1, replica_groups=mesh['z'=8,'core'=2,'x'=4,'y'=4] {'x','y'}, dimensions={0} | all-to-all | bytes 262144 | tf_op jit(solution)/shard_map/all_to_all | solution.py:213
  99.5 4.1 %collective-permute-start.1 = (f32[16,2,8,128]{3,2,1,0:T(8,128)S(1)}, f32[16,2,8,128]{3,2,1,0:T(8,128)S(1)}, u32[]{:S(2)}, u32[]{:S(2)}) collective-permute-start(f32[16,2,8,128]{3,2,1,0:T(8,128)S(1)} %all_to_all.42), channel_id=1, source_target_pairs={{0,16},{16,0},{1,17},{17,1},{2,18},{18,2},{3,19},{19,3},{4,20},{20... | collective-permute-start | bytes 393224 | tf_op jit(solution)/shard_map/ppermute | solution.py:228
  103.7 1.0 collective-permute-done.1
  104.6 7.7 %shard_map.42 = (f32[512,128]{1,0:T(8,128)}, f32[128,1024]{1,0:T(8,128)S(1)}) custom-call(s32[1]{0:T(128)} %bitcast.1.place, f32[64,512]{1,0:T(8,128)S(1)} %bitcast.33, f32[64,512]{1,0:T(8,128)S(1)} %bitcast.35, f32[512,1024]{1,0:T(8,128)S(1)} %bitcast.32), custom_call_target="tpu_custom_call" | custom-call | tf_op jit(solution)/shard_map/pallas_call | solution.py:160
  112.4 20.1 %all_to_all.43 = f32[16,8,1024]{2,1,0:T(8,128)S(1)} all-to-all(f32[16,8,1024]{2,1,0:T(8,128)S(1)} %bitcast.34), channel_id=1, replica_groups=mesh['z'=8,'core'=2,'x'=4,'y'=4] {'z','core'}, dimensions={0} | all-to-all | bytes 1048576 | tf_op jit(solution)/shard_map/all_to_all | solution.py:245
  132.5 0.8 copy.5
  (6 shorter events, 0.1 us)
Async XLA Ops:
  0.6 62.5 %copy-start = (f32[512,128]{1,0:T(8,128)S(1)}, f32[512,128]{1,0:T(8,128)}, u32[]{:S(2)}) copy-start(f32[512,128]{1,0:T(8,128)} %param.3) | copy-start | bytes 786436
  65.1 1.4 %collective-permute-start = (f32[32,8,128]{2,1,0:T(8,128)S(1)}, f32[32,8,128]{2,1,0:T(8,128)S(1)}, u32[]{:S(2)}, u32[]{:S(2)}) collective-permute-start(f32[32,8,128]{2,1,0:T(8,128)S(1)} %dynamic-slice_bitcast_fusion), channel_id=1, source_target_pairs={{0,16},{16,0},{1,17},{17,1},{2,18},{18,2},{3,19},{19,3},{4,20},{20... | collective-permute-start | bytes 393224 | tf_op jit(solution)/shard_map/ppermute | solution.py:223
  99.5 5.1 %collective-permute-start.1 = (f32[16,2,8,128]{3,2,1,0:T(8,128)S(1)}, f32[16,2,8,128]{3,2,1,0:T(8,128)S(1)}, u32[]{:S(2)}, u32[]{:S(2)}) collective-permute-start(f32[16,2,8,128]{3,2,1,0:T(8,128)S(1)} %all_to_all.42), channel_id=1, source_target_pairs={{0,16},{16,0},{1,17},{17,1},{2,18},{18,2},{3,19},{19,3},{4,20},{20... | collective-permute-start | bytes 393224 | tf_op jit(solution)/shard_map/ppermute | solution.py:228

commit v5 on v4

--- a/solution.py
+++ b/solution.py
@@ -232,6 +232,29 @@
     ]
 
 
+def lay_out_kernel(groups, whole, left):
+    members, _, some = groups.shape
+    sends = []
+    for member in range(members):
+        columns = slice(member * some, (member + 1) * some)
+        sends.append(pltpu.make_async_copy(groups.at[member], whole.at[:, columns], left.at[member]))
+        sends[-1].start()
+    for send in sends:
+        send.wait()
+
+
+def lay_out(groups):
+    members, rows, some = groups.shape
+    return pl.pallas_call(
+        lay_out_kernel,
+        out_shape=pltpu.HBM((rows, members * some), jnp.float32),
+        in_specs=[pl.BlockSpec(memory_space=pltpu.VMEM)],
+        out_specs=pl.BlockSpec(memory_space=pl.ANY),
+        scratch_shapes=[pltpu.SemaphoreType.DMA((members,))],
+        compiler_params=pltpu.CompilerParams(vmem_limit_bytes=4 * 2**20),
+    )(in_vmem(groups))
+
+
 def shards(snapshots, start_basis):
     pieces = regroup(snapshots, lax.axis_size(MODE))
     core = lax.axis_index("core")
@@ -242,8 +265,9 @@
     along_cols = close_dot(start_basis, fibres, ((0,), (0,)))
     partial_term = close_dot(along_cols, fibres, ((1,), (1,)))
     basis, core_local = finish(core, *half_sums(partial_term, core), fibres)
-    core_tensor = lax.all_to_all(core_local, MODE, split_axis=0, concat_axis=1, tiled=True)
-    return (basis, core_tensor)
+    groups = core_local.reshape(lax.axis_size(MODE), -1, core_local.shape[1])
+    groups = lax.all_to_all(groups, MODE, 0, 0, tiled=True)
+    return (basis, lay_out(groups))
 
 
 def solution(mesh):

time: 134 us -> 134 us (level)
  no operation moved by 1% of the time
where the time goes in v5:
time: 134 us; the launch traced here: 133 us
  blocking collectives  114 us (85%)
  Pallas kernels  10.4 us (8%)
  starting transfers between devices  4.21 us (3%)
  waiting for transfers between devices  2.32 us (2%)
  matrix products  1.91 us (1%)
    all_to_all x1, blocking collectives, shards(): fibres = lax.all_to_all(pieces, MODE, 0, 0, tiled=True)  60.7 us
    all_to_all x1, blocking collectives, shards(): groups = lax.all_to_all(groups, MODE, 0, 0, tiled=True)  20.1 us
    all_to_all x2, blocking collectives, from_everyone(): return lax.all_to_all(copies, axis, split_axis=0, concat_axis=0, tiled=True)  19.6 us
    all_to_all x1, blocking collectives, half_sums(): own = lax.all_to_all(pieces, COLS, 0, 0, tiled=True).sum(axis=0)  13.3 us
    pallas_call x1, Pallas kernels, finish(): pl.pallas_call(finish_kernel, out_shape=(pltpu.HBM((length, rank), jnp.fl...  7.75 us
    ppermute x1, starting transfers between devices, half_sums(): other = lax.ppermute(half, 'core', swap)  4.11 us
  transfers between devices with their start and end apart: 2, of which 2 were waited for; matrix products, arithmetic and copies ran while one was open for 0% of the time, Pallas kernels for 0%

profile of v5, /device:TPU:1, one launch (start us, length us, event | category | flops | bytes accessed | tf_op | source)
XLA Modules:
  0.0 133.4 jit_solution(6316696421559889080)
XLA Ops:
  0.6 0.0 copy-start
  0.6 1.8 %shard_map.41 = f32[16,32,1024]{2,1,0:T(8,128)S(1)} custom-call(f32[32,16384]{1,0:T(8,128)} %snapshots.1), custom_call_target="tpu_custom_call" | custom-call | tf_op jit(solution)/shard_map/pallas_call | solution.py:201
  2.4 60.7 %all_to_all.25 = f32[16,32,1024]{2,1,0:T(8,128)S(1)} all-to-all(f32[16,32,1024]{2,1,0:T(8,128)S(1)} %shard_map.41), channel_id=1, replica_groups=mesh['z'=8,'core'=2,'x'=4,'y'=4] {'z','core'}, dimensions={0} | all-to-all | bytes 4194304 | tf_op jit(solution)/shard_map/all_to_all | solution.py:262
  63.1 0.0 copy-done
  63.1 0.7 fusion
  63.8 1.2 fusion.1
  65.1 0.1 collective-permute-start
  65.2 1.3 %collective-permute-done = f32[32,8,128]{2,1,0:T(8,128)S(1)} collective-permute-done((f32[32,8,128]{2,1,0:T(8,128)S(1)}, f32[32,8,128]{2,1,0:T(8,128)S(1)}, u32[]{:S(2)}, u32[]{:S(2)}) %collective-permute-start) | collective-permute-done | bytes 131104 | tf_op jit(solution)/shard_map/ppermute | solution.py:223
  66.5 13.3 %all_to_all.26 = f32[16,2,8,128]{3,2,1,0:T(8,128)S(1)} all-to-all(f32[16,2,8,128]{3,2,1,0:T(8,128)S(1)} %bitcast.35), channel_id=1, replica_groups=mesh['z'=8,'core'=2,'x'=4,'y'=4] {'x','y'}, dimensions={0} | all-to-all | bytes 262144 | tf_op jit(solution)/shard_map/all_to_all | solution.py:225
  79.9 9.7 %all_to_all.27 = f32[8,2,8,128]{3,2,1,0:T(8,128)S(1)} all-to-all(f32[8,2,8,128]{3,2,1,0:T(8,128)S(1)} %broadcast_in_dim.10), channel_id=1, replica_groups=mesh['z'=8,'core'=2,'x'=4,'y'=4] {'z'}, dimensions={0} | all-to-all | bytes 131072 | tf_op jit(solution)/shard_map/all_to_all | solution.py:213
  89.6 9.9 %all_to_all.28 = f32[16,2,8,128]{3,2,1,0:T(8,128)S(1)} all-to-all(f32[16,2,8,128]{3,2,1,0:T(8,128)S(1)} %broadcast_in_dim.11), channel_id=1, replica_groups=mesh['z'=8,'core'=2,'x'=4,'y'=4] {'x','y'}, dimensions={0} | all-to-all | bytes 262144 | tf_op jit(solution)/shard_map/all_to_all | solution.py:213
  99.5 4.1 %collective-permute-start.1 = (f32[16,2,8,128]{3,2,1,0:T(8,128)S(1)}, f32[16,2,8,128]{3,2,1,0:T(8,128)S(1)}, u32[]{:S(2)}, u32[]{:S(2)}) collective-permute-start(f32[16,2,8,128]{3,2,1,0:T(8,128)S(1)} %all_to_all.28), channel_id=1, source_target_pairs={{0,16},{16,0},{1,17},{17,1},{2,18},{18,2},{3,19},{19,3},{4,20},{20... | collective-permute-start | bytes 393224 | tf_op jit(solution)/shard_map/ppermute | solution.py:228
  103.7 1.0 collective-permute-done.1
  104.6 7.7 %shard_map.42 = (f32[512,128]{1,0:T(8,128)}, f32[128,1024]{1,0:T(8,128)S(1)}) custom-call(s32[1]{0:T(128)} %bitcast.1.place, f32[64,512]{1,0:T(8,128)S(1)} %bitcast.30, f32[64,512]{1,0:T(8,128)S(1)} %bitcast.32, f32[512,1024]{1,0:T(8,128)S(1)} %bitcast.29), custom_call_target="tpu_custom_call" | custom-call | tf_op jit(solution)/shard_map/pallas_call | solution.py:160
  112.4 20.1 %all_to_all.29.groups = f32[16,8,1024]{2,1,0:T(8,128)S(1)} all-to-all(f32[16,8,1024]{2,1,0:T(8,128)S(1)} %bitcast.31), channel_id=1, replica_groups=mesh['z'=8,'core'=2,'x'=4,'y'=4] {'z','core'}, dimensions={0} | all-to-all | bytes 1048576 | tf_op jit(solution)/shard_map/all_to_all | solution.py:269
  132.5 0.9 shard_map.43
  (6 shorter events, 0.1 us)
Async XLA Ops:
  0.6 62.5 %copy-start = (f32[512,128]{1,0:T(8,128)S(1)}, f32[512,128]{1,0:T(8,128)}, u32[]{:S(2)}) copy-start(f32[512,128]{1,0:T(8,128)} %param.3) | copy-start | bytes 786436
  65.1 1.4 %collective-permute-start = (f32[32,8,128]{2,1,0:T(8,128)S(1)}, f32[32,8,128]{2,1,0:T(8,128)S(1)}, u32[]{:S(2)}, u32[]{:S(2)}) collective-permute-start(f32[32,8,128]{2,1,0:T(8,128)S(1)} %dynamic-slice_bitcast_fusion), channel_id=1, source_target_pairs={{0,16},{16,0},{1,17},{17,1},{2,18},{18,2},{3,19},{19,3},{4,20},{20... | collective-permute-start | bytes 393224 | tf_op jit(solution)/shard_map/ppermute | solution.py:223
  99.5 5.1 %collective-permute-start.1 = (f32[16,2,8,128]{3,2,1,0:T(8,128)S(1)}, f32[16,2,8,128]{3,2,1,0:T(8,128)S(1)}, u32[]{:S(2)}, u32[]{:S(2)}) collective-permute-start(f32[16,2,8,128]{3,2,1,0:T(8,128)S(1)} %all_to_all.28), channel_id=1, source_target_pairs={{0,16},{16,0},{1,17},{17,1},{2,18},{18,2},{3,19},{19,3},{4,20},{20... | collective-permute-start | bytes 393224 | tf_op jit(solution)/shard_map/ppermute | solution.py:228

commit v6 on v4

--- a/solution.py
+++ b/solution.py
@@ -8,6 +8,7 @@
 
 MODE = ("z", "core")
 COLS = ("x", "y")
+PLANE = ("y", "x")
 BLOCK = 8
 PANEL = 64
 CHUNK = 256
@@ -221,10 +222,10 @@
     away = lax.dynamic_index_in_dim(halves, 1 - core, 0, keepdims=False)
     kept = lax.dynamic_index_in_dim(halves, core, 0, keepdims=False)
     kept = kept + lax.ppermute(away, "core", swap)
-    pieces = kept.reshape(lax.axis_size(COLS), -1, 8, LANES)
-    own = lax.all_to_all(pieces, COLS, 0, 0, tiled=True).sum(axis=0)
+    pieces = kept.reshape(lax.axis_size(PLANE), -1, 8, LANES)
+    own = lax.all_to_all(pieces, PLANE, 0, 0, tiled=True).sum(axis=0)
     own = from_everyone(own, "z").sum(axis=0)
-    half = from_everyone(own, COLS)
+    half = from_everyone(own, PLANE)
     other = lax.ppermute(half, "core", swap)
     shape = (rows // 16, lanes // LANES, 8, LANES)
     return [

time: 134 us -> 134 us (level)
  no operation moved by 1% of the time
where the time goes in v6:
time: 134 us; the launch traced here: 133 us
  blocking collectives  114 us (85%)
  Pallas kernels  9.52 us (7%)
  starting transfers between devices  4.21 us (3%)
  waiting for transfers between devices  2.32 us (2%)
  matrix products  1.91 us (1%)
    all_to_all x1, blocking collectives, shards(): fibres = lax.all_to_all(pieces, MODE, 0, 0, tiled=True)  60.7 us
    all_to_all x1, blocking collectives, shards(): lax.all_to_all(core_local, MODE, split_axis=0, concat_axis=1, tiled=True)  20.1 us
    all_to_all x2, blocking collectives, from_everyone(): return lax.all_to_all(copies, axis, split_axis=0, concat_axis=0, tiled=True)  19.5 us
    all_to_all x1, blocking collectives, half_sums(): own = lax.all_to_all(pieces, PLANE, 0, 0, tiled=True).sum(axis=0)  13.4 us
    pallas_call x1, Pallas kernels, finish(): pl.pallas_call(finish_kernel, out_shape=(pltpu.HBM((length, rank), jnp.fl...  7.75 us
    ppermute x1, starting transfers between devices, half_sums(): other = lax.ppermute(half, 'core', swap)  4.11 us
  transfers between devices with their start and end apart: 2, of which 2 were waited for; matrix products, arithmetic and copies ran while one was open for 0% of the time, Pallas kernels for 0%

profile of v6, /device:TPU:1, one launch (start us, length us, event | category | flops | bytes accessed | tf_op | source)
XLA Modules:
  0.0 133.3 jit_solution(17706958152175497192)
XLA Ops:
  0.6 0.0 copy-start
  0.6 1.8 %shard_map.41 = f32[16,32,1024]{2,1,0:T(8,128)S(1)} custom-call(f32[32,16384]{1,0:T(8,128)} %snapshots.1), custom_call_target="tpu_custom_call" | custom-call | tf_op jit(solution)/shard_map/pallas_call | solution.py:202
  2.4 60.7 %all_to_all.39 = f32[16,32,1024]{2,1,0:T(8,128)S(1)} all-to-all(f32[16,32,1024]{2,1,0:T(8,128)S(1)} %shard_map.41), channel_id=1, replica_groups=mesh['z'=8,'core'=2,'x'=4,'y'=4] {'z','core'}, dimensions={0} | all-to-all | bytes 4194304 | tf_op jit(solution)/shard_map/all_to_all | solution.py:240
  63.1 0.0 copy-done
  63.1 0.7 fusion
  63.8 1.2 fusion.1
  65.1 0.1 collective-permute-start
  65.2 1.3 %collective-permute-done = f32[32,8,128]{2,1,0:T(8,128)S(1)} collective-permute-done((f32[32,8,128]{2,1,0:T(8,128)S(1)}, f32[32,8,128]{2,1,0:T(8,128)S(1)}, u32[]{:S(2)}, u32[]{:S(2)}) %collective-permute-start) | collective-permute-done | bytes 131104 | tf_op jit(solution)/shard_map/ppermute | solution.py:224
  66.5 13.4 %all_to_all.40 = f32[16,2,8,128]{3,2,1,0:T(8,128)S(1)} all-to-all(f32[16,2,8,128]{3,2,1,0:T(8,128)S(1)} %bitcast.39), channel_id=1, replica_groups=mesh['z'=8,'core'=2,'x'=4,'y'=4] {'y','x'}, dimensions={0} | all-to-all | bytes 262144 | tf_op jit(solution)/shard_map/all_to_all | solution.py:226
  80.0 9.7 %all_to_all.41 = f32[8,2,8,128]{3,2,1,0:T(8,128)S(1)} all-to-all(f32[8,2,8,128]{3,2,1,0:T(8,128)S(1)} %broadcast_in_dim.10), channel_id=1, replica_groups=mesh['z'=8,'core'=2,'x'=4,'y'=4] {'z'}, dimensions={0} | all-to-all | bytes 131072 | tf_op jit(solution)/shard_map/all_to_all | solution.py:214
  89.7 9.8 %all_to_all.42 = f32[16,2,8,128]{3,2,1,0:T(8,128)S(1)} all-to-all(f32[16,2,8,128]{3,2,1,0:T(8,128)S(1)} %broadcast_in_dim.11), channel_id=1, replica_groups=mesh['z'=8,'core'=2,'x'=4,'y'=4] {'y','x'}, dimensions={0} | all-to-all | bytes 262144 | tf_op jit(solution)/shard_map/all_to_all | solution.py:214
  99.5 4.1 %collective-permute-start.1 = (f32[16,2,8,128]{3,2,1,0:T(8,128)S(1)}, f32[16,2,8,128]{3,2,1,0:T(8,128)S(1)}, u32[]{:S(2)}, u32[]{:S(2)}) collective-permute-start(f32[16,2,8,128]{3,2,1,0:T(8,128)S(1)} %all_to_all.42), channel_id=1, source_target_pairs={{0,16},{16,0},{1,17},{17,1},{2,18},{18,2},{3,19},{19,3},{4,20},{20... | collective-permute-start | bytes 393224 | tf_op jit(solution)/shard_map/ppermute | solution.py:229
  103.6 1.0 collective-permute-done.1
  104.6 7.7 %shard_map.42 = (f32[512,128]{1,0:T(8,128)}, f32[128,1024]{1,0:T(8,128)S(1)}) custom-call(s32[1]{0:T(128)} %bitcast.1.place, f32[64,512]{1,0:T(8,128)S(1)} %bitcast.33, f32[64,512]{1,0:T(8,128)S(1)} %bitcast.35, f32[512,1024]{1,0:T(8,128)S(1)} %bitcast.32), custom_call_target="tpu_custom_call" | custom-call | tf_op jit(solution)/shard_map/pallas_call | solution.py:161
  112.4 20.1 %all_to_all.43 = f32[16,8,1024]{2,1,0:T(8,128)S(1)} all-to-all(f32[16,8,1024]{2,1,0:T(8,128)S(1)} %bitcast.34), channel_id=1, replica_groups=mesh['z'=8,'core'=2,'x'=4,'y'=4] {'z','core'}, dimensions={0} | all-to-all | bytes 1048576 | tf_op jit(solution)/shard_map/all_to_all | solution.py:246
  132.5 0.8 copy.5
  (6 shorter events, 0.1 us)
Async XLA Ops:
  0.6 62.5 %copy-start = (f32[512,128]{1,0:T(8,128)S(1)}, f32[512,128]{1,0:T(8,128)}, u32[]{:S(2)}) copy-start(f32[512,128]{1,0:T(8,128)} %param.3) | copy-start | bytes 786436
  65.1 1.4 %collective-permute-start = (f32[32,8,128]{2,1,0:T(8,128)S(1)}, f32[32,8,128]{2,1,0:T(8,128)S(1)}, u32[]{:S(2)}, u32[]{:S(2)}) collective-permute-start(f32[32,8,128]{2,1,0:T(8,128)S(1)} %dynamic-slice_bitcast_fusion), channel_id=1, source_target_pairs={{0,16},{16,0},{1,17},{17,1},{2,18},{18,2},{3,19},{19,3},{4,20},{20... | collective-permute-start | bytes 393224 | tf_op jit(solution)/shard_map/ppermute | solution.py:224
  99.5 5.1 %collective-permute-start.1 = (f32[16,2,8,128]{3,2,1,0:T(8,128)S(1)}, f32[16,2,8,128]{3,2,1,0:T(8,128)S(1)}, u32[]{:S(2)}, u32[]{:S(2)}) collective-permute-start(f32[16,2,8,128]{3,2,1,0:T(8,128)S(1)} %all_to_all.42), channel_id=1, source_target_pairs={{0,16},{16,0},{1,17},{17,1},{2,18},{18,2},{3,19},{19,3},{4,20},{20... | collective-permute-start | bytes 393224 | tf_op jit(solution)/shard_map/ppermute | solution.py:229
